TPU v7x, 32 devices: a whole 2x2x4 slice. The times are simulated.
32 devices in a mesh: grp: 2 (over y), row: 8 (over z, x), col: 2 (over core).
Axes of the slice: x: 2, y: 2, z: 4, core: 2. Of those that a mesh axis runs over, the one named last changes fastest.
Arguments:
- pair_feats: float32 [32, 16, 192], P(('grp', 'row'), 'col'), parts along dimension 0, may hold values from -6 to 6
- pair_class: int32 [32, 16], P(('grp', 'row'), 'col'), parts along dimension 0, may hold values from 0 to 63
- class_table: float32 [64, 192], replicated, may hold values from -4 to 4
- kernel_one: bfloat16 [3, 3, 192, 192], replicated, may hold values from -0.15625 to 0.15625
- kernel_two: bfloat16 [3, 3, 192, 192], replicated, may hold values from -0.15625 to 0.15625
- norm_gain: float32 [192], replicated, may hold values from 0.1 to 1.9
- w_in: bfloat16 [384, 768], replicated, may hold values from -0.3125 to 0.3125
- w_out: bfloat16 [768, 384], replicated, may hold values from -0.21875 to 0.21875
- partner_perm: int32 [4, 16], replicated, may hold values from 0 to 15, each once within a row
Outputs:
- pair_out: float32 [32, 16, 192], P(('grp', 'row'), 'col'), parts along dimension 0
There are 2 independent parts, one for each index of `grp`. A program takes and returns all parts, laid end to end along the dimension named above; an argument that names none is the same for every part. Nothing has to cross between parts.
Inputs may be any that keep to these rules, and one draw needn't show every extreme that they name: `partner_perm`: each row is a permutation of the 16 cells of a tile.
All inputs are finite; a program needn't handle non-finite values.
Results may differ from a plain program's by a relative error of at most 0.005.
Values may be sent and summed in bfloat16 or wider, within the bound.
A program may use at most 64 MiB of HBM per device.

v0:
```python
import jax
import jax.numpy as jnp
from jax import lax
from jax.sharding import PartitionSpec as P


def with_halo(x, sides, width):
    for axis, dim in sides:
        size, length = (lax.axis_size(axis), x.shape[dim])
        up = [(i, (i + 1) % size) for i in range(size - 1)]
        down = [(j, i) for i, j in up]
        last = lax.slice_in_dim(x, length - width, length, axis=dim)
        first = lax.slice_in_dim(x, 0, width, axis=dim)
        before = lax.ppermute(last, axis, up)
        after = lax.ppermute(first, axis, down)
        x = jnp.concatenate([before, x, after], axis=dim)
    return x


def swapped(block, axis, apart):
    count = lax.axis_size(axis)
    route = []
    for low in range(count):
        high = low | 1 << apart
        if high != low and high < count:
            route += [(low, high), (high, low)]
    return lax.ppermute(block, axis, route)


def convolve(values, kernel):
    tile_rows, tile_cols, channels = values.shape
    padded = with_halo(values, (("row", 0), ("col", 1)), 1)
    summed = jnp.zeros((tile_rows * tile_cols, kernel.shape[3]), jnp.float32)
    for row_shift in range(3):
        for col_shift in range(3):
            window = padded[
                row_shift : row_shift + tile_rows, col_shift : col_shift + tile_cols
            ].reshape(tile_rows * tile_cols, channels)
            summed = summed + jnp.dot(
                window, kernel[row_shift, col_shift], preferred_element_type=jnp.float32
            )
    return jnp.maximum(summed, 0.0)


def axis_position(axis_name):
    if axis_name == "row":
        return lax.axis_index("row")
    return lax.axis_index("col")


def trade_normed(values, axis_name, bit_index):
    if axis_name == "row":
        return swapped(values, "row", bit_index)
    return swapped(values, "col", bit_index)


def switch_level(stream, axis_name, bit_index, order, norm_gain, w_in, w_out):
    cell_count, channels = stream.shape
    upper_flag = axis_position(axis_name) >> bit_index & 1
    is_upper = upper_flag == 1
    scaled = (
        stream * lax.rsqrt(jnp.mean(stream * stream, axis=-1, keepdims=True) + 1e-05) * norm_gain
    )
    normed = scaled.astype(jnp.bfloat16)
    partner = trade_normed(normed, axis_name, bit_index)
    lower_part = jnp.where(is_upper, partner, normed)
    upper_part = jnp.where(is_upper, normed, partner)
    pair_units = jnp.concatenate([lower_part, upper_part[order]], axis=1)
    hidden = jnp.maximum(jnp.dot(pair_units, w_in, preferred_element_type=jnp.float32), 0.0).astype(
        jnp.bfloat16
    )
    out_cols = lax.dynamic_slice_in_dim(w_out, upper_flag * channels, channels, 1)
    update = jnp.dot(hidden, out_cols, preferred_element_type=jnp.float32)
    inverse = jnp.zeros_like(order).at[order].set(jnp.arange(cell_count, dtype=jnp.int32))
    update = jnp.where(is_upper, update[inverse], update)
    return stream + update


def per_device(
    pair_feats,
    pair_class,
    class_table,
    kernel_one,
    kernel_two,
    norm_gain,
    w_in,
    w_out,
    partner_perm,
):
    tile_rows, tile_cols, channels = pair_feats.shape
    cell_count = tile_rows * tile_cols
    class_count = class_table.shape[0]
    onehot = (
        pair_class.reshape(cell_count, 1) == jnp.arange(class_count, dtype=jnp.int32)[None, :]
    ).astype(jnp.float32)
    embedded = jnp.dot(onehot, class_table, precision=lax.Precision.HIGHEST)
    initial = pair_feats.reshape(cell_count, channels) + embedded
    conv_one = convolve(
        initial.astype(jnp.bfloat16).reshape(tile_rows, tile_cols, channels), kernel_one
    )
    conv_one = conv_one.astype(jnp.bfloat16).reshape(tile_rows, tile_cols, channels)
    stream = initial + convolve(conv_one, kernel_two)
    row_bits = lax.axis_size("row").bit_length() - 1
    level_index = 0
    for bit_index in range(row_bits):
        stream = switch_level(
            stream, "row", bit_index, partner_perm[level_index], norm_gain, w_in, w_out
        )
        level_index = level_index + 1
    bit_index = 0
    stream = switch_level(
        stream, "col", bit_index, partner_perm[level_index], norm_gain, w_in, w_out
    )
    return stream.reshape(tile_rows, tile_cols, channels)


def solution(mesh):
    return jax.shard_map(
        per_device,
        mesh=mesh,
        in_specs=(
            P(("grp", "row"), "col", None),
            P(("grp", "row"), "col"),
            P(),
            P(),
            P(),
            P(),
            P(),
            P(),
            P(),
        ),
        out_specs=P(("grp", "row"), "col", None),
        check_vma=False,
    )
```

profile of v0, /device:TPU:0, one launch (start us, length us, event | category | flops | bytes accessed | tf_op | source)
XLA Modules:
  0.0 64.5 jit_solution(8228434552011810848)
XLA Ops:
  0.0 0.9 %eq.27 = s32[16]{0:T(128)S(1)} reshape(s32[2,8]{1,0:T(2,128)} %param.10) | data formatting | bytes 128 | tf_op jit(solution)/shard_map/eq | solution.py:94
  0.9 1.0 %fusion.223 = (bf16[16,192]{1,0:T(8,128)(2,1)S(1)}, f32[16,192]{1,0:T(8,128)S(1)}) fusion(f32[64,192]{1,0:T(8,128)} %param.11, s32[16]{0:T(128)S(1)} %eq.27, f32[2,8,192]{2,1,0:T(8,128)} %param.9), kind=kOutput, calls=%fused_computation.295 | convolution fusion | flops 2366464 | bytes 79936 | tf_op jit(solution)/shard_map/dot_general | solution.py:96
  1.9 4.8 %collective-permute-start = (bf16[1,8,192]{2,1,0:T(8,128)(2,1)S(1)}, bf16[1,8,192]{2,1,0:T(8,128)(2,1)S(1)}, u32[]{:S(2)}, u32[]{:S(2)}) collective-permute-start(bf16[1,8,192]{2,1,0:T(8,128)(2,1)S(1)} %get-tuple-element.25), channel_id=1, source_target_pairs={{0,2},{2,4},{4,6},{6,8},{8,10},{10,12},{12,14},{1,3},{3,5},{5,7},{... | collective-permute-start | bytes 9224 | tf_op jit(solution)/shard_map/ppermute | solution.py:14
  6.8 1.3 %collective-permute-start.1 = (bf16[1,8,192]{2,1,0:T(8,128)(2,1)S(1)}, bf16[1,8,192]{2,1,0:T(8,128)(2,1)S(1)}, u32[]{:S(2)}, u32[]{:S(2)}) collective-permute-start(bf16[1,8,192]{2,1,0:T(8,128)(2,1)S(1)} %get-tuple-element.26), channel_id=1, source_target_pairs={{2,0},{4,2},{6,4},{8,6},{10,8},{12,10},{14,12},{3,1},{5,3},{7,5},{... | collective-permute-start | bytes 9224 | tf_op jit(solution)/shard_map/ppermute | solution.py:15
  8.1 1.0 %fusion.51 = f32[16,192]{1,0:T(8,128)S(1)} fusion(bf16[16,192]{1,0:T(8,128)(2,1)S(1)} %get-tuple-element.31, bf16[3,3,192,192]{3,2,1,0:T(8,128)(2,1)} %param.12), kind=kOutput, calls=%fused_computation.72 | convolution fusion | flops 1179648 | bytes 116736 | tf_op jit(solution)/shard_map/dot_general | solution.py:39
  9.1 0.8 %fusion.186 = (s32[16]{0:T(128)S(1)}, s32[16]{0:T(128)S(1)}, s32[16]{0:T(128)S(1)}, s32[16]{0:T(128)S(1)}) fusion(s32[4,16]{1,0:T(4,128)} %param.17), kind=kLoop, calls=%fused_computation.258 | loop fusion | flops 192 | bytes 512 | tf_op jit(solution)/shard_map/select_n | solution.py:68
  10.0 0.6 scatter_custom_fusion
  10.6 0.6 scatter_custom_fusion.1
  11.3 0.6 scatter_custom_fusion.2
  11.9 0.6 scatter_custom_fusion.3
  12.6 1.3 %collective-permute-start.3 = (bf16[4,1,192]{2,1,0:T(2,128)(2,1)S(1)}, bf16[4,1,192]{2,1,0:T(2,128)(2,1)S(1)}, u32[]{:S(2)}, u32[]{:S(2)}) collective-permute-start(bf16[4,1,192]{2,1,0:T(2,128)(2,1)S(1)} %get-tuple-element.22), channel_id=1, source_target_pairs={{1,0},{3,2},{5,4},{7,6},{9,8},{11,10},{13,12},{15,14},{17,16},{19,... | collective-permute-start | bytes 4616 | tf_op jit(solution)/shard_map/ppermute | solution.py:15
  13.9 3.0 %collective-permute-start.2 = (bf16[4,1,192]{2,1,0:T(2,128)(2,1)S(1)}, bf16[4,1,192]{2,1,0:T(2,128)(2,1)S(1)}, u32[]{:S(2)}, u32[]{:S(2)}) collective-permute-start(bf16[4,1,192]{2,1,0:T(2,128)(2,1)S(1)} %get-tuple-element.21), channel_id=1, source_target_pairs={{0,1},{2,3},{4,5},{6,7},{8,9},{10,11},{12,13},{14,15},{16,17},{18,... | collective-permute-start | bytes 4616 | tf_op jit(solution)/shard_map/ppermute | solution.py:14
  17.0 1.0 %fusion.57 = f32[16,192]{1,0:T(8,128)S(1)} fusion(bf16[3,3,192,192]{3,2,1,0:T(8,128)(2,1)} %param.12, bf16[2,8,192]{2,1,0:T(8,128)(2,1)S(1)} %bitcast.144, bf16[1,8,192]{2,1,0:T(8,128)(2,1)S(1)} %collective-permute-done), kind=kOutput, calls=%fused_computation.78 | convolution fusion | flops 1182720 | bytes 119808 | tf_op jit(solution)/shard_map/dot_general | solution.py:39
  18.0 1.0 %fusion.46 = f32[16,192]{1,0:T(8,128)S(1)} fusion(bf16[3,3,192,192]{3,2,1,0:T(8,128)(2,1)} %param.12, bf16[1,8,192]{2,1,0:T(8,128)(2,1)S(1)} %collective-permute-done.1, bf16[2,8,192]{2,1,0:T(8,128)(2,1)S(1)} %bitcast.145), kind=kOutput, calls=%fused_computation.67 | convolution fusion | flops 1182720 | bytes 119808 | tf_op jit(solution)/shard_map/dot_general | solution.py:39
  19.0 1.0 %fusion.53 = f32[16,192]{1,0:T(8,128)S(1)} fusion(bf16[3,3,192,192]{3,2,1,0:T(8,128)(2,1)} %param.12, bf16[4,1,192]{2,1,0:T(2,128)(2,1)S(1)} %collective-permute-done.2, bf16[1,8,192]{2,1,0:T(8,128)(2,1)S(1)} %collective-permute-done.1, bf16[2,8,192]{2,1,0:T(8,128)(2,1)S(1)} %bitcast.146, bf16[1,8,192]{2,1,0:T(8,128)(2,1)S(1)} %collective-permute-done), kind=kOutput, calls=%fused_computation.74 | convolution fusion | flops 1204224 | bytes 124416 | tf_op jit(solution)/shard_map/dot_general | solution.py:39
  20.1 1.0 %fusion.48 = f32[16,192]{1,0:T(8,128)S(1)} fusion(bf16[3,3,192,192]{3,2,1,0:T(8,128)(2,1)} %param.12, bf16[4,1,192]{2,1,0:T(2,128)(2,1)S(1)} %collective-permute-done.2, bf16[1,8,192]{2,1,0:T(8,128)(2,1)S(1)} %collective-permute-done.1, bf16[2,8,192]{2,1,0:T(8,128)(2,1)S(1)} %bitcast.147, bf16[1,8,192]{2,1,0:T(8,128)(2,1)S(1)} %collective-permute-done), kind=kOutput, calls=%fused_computation.69 | convolution fusion | flops 1204224 | bytes 124416 | tf_op jit(solution)/shard_map/dot_general | solution.py:39
  21.1 1.0 %fusion.55 = f32[16,192]{1,0:T(8,128)S(1)} fusion(bf16[3,3,192,192]{3,2,1,0:T(8,128)(2,1)} %param.12, bf16[4,1,192]{2,1,0:T(2,128)(2,1)S(1)} %collective-permute-done.3, bf16[1,8,192]{2,1,0:T(8,128)(2,1)S(1)} %collective-permute-done.1, bf16[2,8,192]{2,1,0:T(8,128)(2,1)S(1)} %bitcast.148, bf16[1,8,192]{2,1,0:T(8,128)(2,1)S(1)} %collective-permute-done), kind=kOutput, calls=%fused_computation.76 | convolution fusion | flops 1204224 | bytes 124416 | tf_op jit(solution)/shard_map/dot_general | solution.py:39
  22.2 1.0 %fusion.44 = f32[16,192]{1,0:T(8,128)S(1)} fusion(bf16[3,3,192,192]{3,2,1,0:T(8,128)(2,1)} %param.12, bf16[4,1,192]{2,1,0:T(2,128)(2,1)S(1)} %collective-permute-done.3, bf16[1,8,192]{2,1,0:T(8,128)(2,1)S(1)} %collective-permute-done.1, bf16[2,8,192]{2,1,0:T(8,128)(2,1)S(1)} %bitcast.149, bf16[1,8,192]{2,1,0:T(8,128)(2,1)S(1)} %collective-permute-done), kind=kOutput, calls=%fused_computation.65 | convolution fusion | flops 1204224 | bytes 124416 | tf_op jit(solution)/shard_map/dot_general | solution.py:39
  23.2 1.0 %fusion.22 = f32[16,192]{1,0:T(8,128)S(1)} fusion(f32[16,192]{1,0:T(8,128)S(1)} %fusion.51, f32[16,192]{1,0:T(8,128)S(1)} %fusion.53, f32[16,192]{1,0:T(8,128)S(1)} %fusion.55, f32[16,192]{1,0:T(8,128)S(1)} %fusion.57, bf16[3,3,192,192]{3,2,1,0:T(8,128)(2,1)} %param.12, bf16[4,1,192]{2,1,0:T(2,128)(2,1)S(1)} %collective-permute-done.2, ...), kind=kOutput, calls=%fused_computation.42 | convolution fusion | flops 1216512 | bytes 173568 | tf_op jit(solution)/shard_map/dot_general | solution.py:39
  24.2 1.0 %fusion.23 = bf16[16,192]{1,0:T(8,128)(2,1)S(1)} fusion(f32[16,192]{1,0:T(8,128)S(1)} %fusion.44, f32[16,192]{1,0:T(8,128)S(1)} %fusion.46, f32[16,192]{1,0:T(8,128)S(1)} %fusion.48, f32[16,192]{1,0:T(8,128)S(1)} %fusion.22, bf16[3,3,192,192]{3,2,1,0:T(8,128)(2,1)} %param.12, bf16[4,1,192]{2,1,0:T(2,128)(2,1)S(1)} %collective-permute-done.3, ...), kind=kOutput, calls=%fused_computation.44 | convolution fusion | flops 1222656 | bytes 167424 | tf_op jit(solution)/shard_map/dot_general | solution.py:39
  25.3 4.5 %collective-permute-start.4 = (bf16[1,8,192]{2,1,0:T(8,128)(2,1)S(1)}, bf16[1,8,192]{2,1,0:T(8,128)(2,1)S(1)}, u32[]{:S(2)}, u32[]{:S(2)}) collective-permute-start(bf16[1,8,192]{2,1,0:T(8,128)(2,1)S(1)} %get-tuple-element.23), channel_id=1, source_target_pairs={{0,2},{2,4},{4,6},{6,8},{8,10},{10,12},{12,14},{1,3},{3,5},{5,7},{... | collective-permute-start | bytes 9224 | tf_op jit(solution)/shard_map/ppermute | solution.py:14
  29.8 1.3 %collective-permute-start.5 = (bf16[1,8,192]{2,1,0:T(8,128)(2,1)S(1)}, bf16[1,8,192]{2,1,0:T(8,128)(2,1)S(1)}, u32[]{:S(2)}, u32[]{:S(2)}) collective-permute-start(bf16[1,8,192]{2,1,0:T(8,128)(2,1)S(1)} %get-tuple-element.24), channel_id=1, source_target_pairs={{2,0},{4,2},{6,4},{8,6},{10,8},{12,10},{14,12},{3,1},{5,3},{7,5},{... | collective-permute-start | bytes 9224 | tf_op jit(solution)/shard_map/ppermute | solution.py:15
  31.3 4.5 %collective-permute-done.5 = bf16[1,8,192]{2,1,0:T(8,128)(2,1)S(1)} collective-permute-done((bf16[1,8,192]{2,1,0:T(8,128)(2,1)S(1)}, bf16[1,8,192]{2,1,0:T(8,128)(2,1)S(1)}, u32[]{:S(2)}, u32[]{:S(2)}) %collective-permute-start.5) | collective-permute-done | bytes 3104 | tf_op jit(solution)/shard_map/ppermute | solution.py:15
  35.8 1.3 %collective-permute-start.7 = (bf16[4,1,192]{2,1,0:T(2,128)(2,1)S(1)}, bf16[4,1,192]{2,1,0:T(2,128)(2,1)S(1)}, u32[]{:S(2)}, u32[]{:S(2)}) collective-permute-start(bf16[4,1,192]{2,1,0:T(2,128)(2,1)S(1)} %get-tuple-element.20), channel_id=1, source_target_pairs={{1,0},{3,2},{5,4},{7,6},{9,8},{11,10},{13,12},{15,14},{17,16},{19,... | collective-permute-start | bytes 4616 | tf_op jit(solution)/shard_map/ppermute | solution.py:15
  37.1 3.0 %collective-permute-start.6 = (bf16[4,1,192]{2,1,0:T(2,128)(2,1)S(1)}, bf16[4,1,192]{2,1,0:T(2,128)(2,1)S(1)}, u32[]{:S(2)}, u32[]{:S(2)}) collective-permute-start(bf16[4,1,192]{2,1,0:T(2,128)(2,1)S(1)} %get-tuple-element.19), channel_id=1, source_target_pairs={{0,1},{2,3},{4,5},{6,7},{8,9},{10,11},{12,13},{14,15},{16,17},{18,... | collective-permute-start | bytes 4616 | tf_op jit(solution)/shard_map/ppermute | solution.py:14
  40.4 0.5 collective-permute-done.6
  41.6 0.3 multiply_reduce_fusion.3
  41.9 0.7 %copy-done.3 = f32[192]{0:T(256)S(1)} copy-done((f32[192]{0:T(256)S(1)}, f32[192]{0:T(256)}, u32[]{:S(2)}) %copy-start.3) | copy-done | bytes 792
  42.7 2.9 %collective-permute-start.8 = (bf16[16,192]{1,0:T(8,128)(2,1)S(1)}, bf16[16,192]{1,0:T(8,128)(2,1)S(1)}, u32[]{:S(2)}, u32[]{:S(2)}) collective-permute-start(bf16[16,192]{1,0:T(8,128)(2,1)S(1)} %multiply_convert_fusion.3), channel_id=1, source_target_pairs={{0,2},{2,0},{4,6},{6,4},{8,10},{10,8},{12,14},{14,12},{1,3},{3,1},... | collective-permute-start | bytes 18440 | tf_op jit(solution)/shard_map/ppermute | solution.py:27
  45.6 1.6 %collective-permute-done.8 = bf16[16,192]{1,0:T(8,128)(2,1)S(1)} collective-permute-done((bf16[16,192]{1,0:T(8,128)(2,1)S(1)}, bf16[16,192]{1,0:T(8,128)(2,1)S(1)}, u32[]{:S(2)}, u32[]{:S(2)}) %collective-permute-start.8) | collective-permute-done | bytes 6176 | tf_op jit(solution)/shard_map/ppermute | solution.py:27
  47.3 0.6 gather_fusion
  47.9 0.4 fusion.7
  48.3 0.6 gather_fusion.1
  49.1 1.6 %collective-permute-start.9 = (bf16[16,192]{1,0:T(8,128)(2,1)S(1)}, bf16[16,192]{1,0:T(8,128)(2,1)S(1)}, u32[]{:S(2)}, u32[]{:S(2)}) collective-permute-start(bf16[16,192]{1,0:T(8,128)(2,1)S(1)} %multiply_convert_fusion.2), channel_id=1, source_target_pairs={{0,4},{4,0},{2,6},{6,2},{8,12},{12,8},{10,14},{14,10},{1,5},{5,1},... | collective-permute-start | bytes 18440 | tf_op jit(solution)/shard_map/ppermute | solution.py:27
  50.7 2.1 %collective-permute-done.9 = bf16[16,192]{1,0:T(8,128)(2,1)S(1)} collective-permute-done((bf16[16,192]{1,0:T(8,128)(2,1)S(1)}, bf16[16,192]{1,0:T(8,128)(2,1)S(1)}, u32[]{:S(2)}, u32[]{:S(2)}) %collective-permute-start.9) | collective-permute-done | bytes 6176 | tf_op jit(solution)/shard_map/ppermute | solution.py:27
  52.8 0.6 gather_fusion.2
  53.4 0.4 fusion.6
  53.8 0.6 gather_fusion.3
  54.6 2.6 %collective-permute-start.10 = (bf16[16,192]{1,0:T(8,128)(2,1)S(1)}, bf16[16,192]{1,0:T(8,128)(2,1)S(1)}, u32[]{:S(2)}, u32[]{:S(2)}) collective-permute-start(bf16[16,192]{1,0:T(8,128)(2,1)S(1)} %multiply_convert_fusion.1), channel_id=1, source_target_pairs={{0,8},{8,0},{2,10},{10,2},{4,12},{12,4},{6,14},{14,6},{1,9},{9,1},... | collective-permute-start | bytes 18440 | tf_op jit(solution)/shard_map/ppermute | solution.py:27
  57.2 2.0 %collective-permute-done.10 = bf16[16,192]{1,0:T(8,128)(2,1)S(1)} collective-permute-done((bf16[16,192]{1,0:T(8,128)(2,1)S(1)}, bf16[16,192]{1,0:T(8,128)(2,1)S(1)}, u32[]{:S(2)}, u32[]{:S(2)}) %collective-permute-start.10) | collective-permute-done | bytes 6176 | tf_op jit(solution)/shard_map/ppermute | solution.py:27
  59.3 0.6 gather_fusion.4
  59.9 0.4 fusion.5
  60.3 0.6 gather_fusion.5
  61.1 1.1 %collective-permute-done.11 = bf16[16,192]{1,0:T(8,128)(2,1)S(1)} collective-permute-done((bf16[16,192]{1,0:T(8,128)(2,1)S(1)}, bf16[16,192]{1,0:T(8,128)(2,1)S(1)}, u32[]{:S(2)}, u32[]{:S(2)}) %collective-permute-start.11) | collective-permute-done | bytes 6176 | tf_op jit(solution)/shard_map/ppermute | solution.py:27
  62.3 0.6 gather_fusion.6
  62.9 0.4 fusion.4
  63.3 0.6 gather_fusion.7
  63.9 0.6 add_bitcast_fusion
  (57 shorter events, 2.2 us)
Async XLA Ops:
  0.0 47.9 %copy-start = (bf16[384,768]{1,0:T(8,128)(2,1)S(1)}, bf16[384,768]{1,0:T(8,128)(2,1)}, u32[]{:S(2)}) copy-start(bf16[384,768]{1,0:T(8,128)(2,1)} %param.15) | copy-start | bytes 1769476
  0.0 31.1 %copy-start.2 = (bf16[3,3,192,192]{3,2,1,0:T(8,128)(2,1)S(1)}, bf16[3,3,192,192]{3,2,1,0:T(8,128)(2,1)}, u32[]{:S(2)}) copy-start(bf16[3,3,192,192]{3,2,1,0:T(8,128)(2,1)} %param.13) | copy-start | bytes 1990660
  1.9 10.7 %collective-permute-start = (bf16[1,8,192]{2,1,0:T(8,128)(2,1)S(1)}, bf16[1,8,192]{2,1,0:T(8,128)(2,1)S(1)}, u32[]{:S(2)}, u32[]{:S(2)}) collective-permute-start(bf16[1,8,192]{2,1,0:T(8,128)(2,1)S(1)} %get-tuple-element.25), channel_id=1, source_target_pairs={{0,2},{2,4},{4,6},{6,8},{8,10},{10,12},{12,14},{1,3},{3,5},{5,7},{... | collective-permute-start | bytes 9224 | tf_op jit(solution)/shard_map/ppermute | solution.py:14
  6.8 5.8 %collective-permute-start.1 = (bf16[1,8,192]{2,1,0:T(8,128)(2,1)S(1)}, bf16[1,8,192]{2,1,0:T(8,128)(2,1)S(1)}, u32[]{:S(2)}, u32[]{:S(2)}) collective-permute-start(bf16[1,8,192]{2,1,0:T(8,128)(2,1)S(1)} %get-tuple-element.26), channel_id=1, source_target_pairs={{2,0},{4,2},{6,4},{8,6},{10,8},{12,10},{14,12},{3,1},{5,3},{7,5},{... | collective-permute-start | bytes 9224 | tf_op jit(solution)/shard_map/ppermute | solution.py:15
  12.6 8.5 %collective-permute-start.3 = (bf16[4,1,192]{2,1,0:T(2,128)(2,1)S(1)}, bf16[4,1,192]{2,1,0:T(2,128)(2,1)S(1)}, u32[]{:S(2)}, u32[]{:S(2)}) collective-permute-start(bf16[4,1,192]{2,1,0:T(2,128)(2,1)S(1)} %get-tuple-element.22), channel_id=1, source_target_pairs={{1,0},{3,2},{5,4},{7,6},{9,8},{11,10},{13,12},{15,14},{17,16},{19,... | collective-permute-start | bytes 4616 | tf_op jit(solution)/shard_map/ppermute | solution.py:15
  13.9 5.1 %collective-permute-start.2 = (bf16[4,1,192]{2,1,0:T(2,128)(2,1)S(1)}, bf16[4,1,192]{2,1,0:T(2,128)(2,1)S(1)}, u32[]{:S(2)}, u32[]{:S(2)}) collective-permute-start(bf16[4,1,192]{2,1,0:T(2,128)(2,1)S(1)} %get-tuple-element.21), channel_id=1, source_target_pairs={{0,1},{2,3},{4,5},{6,7},{8,9},{10,11},{12,13},{14,15},{16,17},{18,... | collective-permute-start | bytes 4616 | tf_op jit(solution)/shard_map/ppermute | solution.py:14
  25.3 6.0 %collective-permute-start.4 = (bf16[1,8,192]{2,1,0:T(8,128)(2,1)S(1)}, bf16[1,8,192]{2,1,0:T(8,128)(2,1)S(1)}, u32[]{:S(2)}, u32[]{:S(2)}) collective-permute-start(bf16[1,8,192]{2,1,0:T(8,128)(2,1)S(1)} %get-tuple-element.23), channel_id=1, source_target_pairs={{0,2},{2,4},{4,6},{6,8},{8,10},{10,12},{12,14},{1,3},{3,5},{5,7},{... | collective-permute-start | bytes 9224 | tf_op jit(solution)/shard_map/ppermute | solution.py:14
  29.8 5.9 %collective-permute-start.5 = (bf16[1,8,192]{2,1,0:T(8,128)(2,1)S(1)}, bf16[1,8,192]{2,1,0:T(8,128)(2,1)S(1)}, u32[]{:S(2)}, u32[]{:S(2)}) collective-permute-start(bf16[1,8,192]{2,1,0:T(8,128)(2,1)S(1)} %get-tuple-element.24), channel_id=1, source_target_pairs={{2,0},{4,2},{6,4},{8,6},{10,8},{12,10},{14,12},{3,1},{5,3},{7,5},{... | collective-permute-start | bytes 9224 | tf_op jit(solution)/shard_map/ppermute | solution.py:15
  35.8 5.4 %collective-permute-start.7 = (bf16[4,1,192]{2,1,0:T(2,128)(2,1)S(1)}, bf16[4,1,192]{2,1,0:T(2,128)(2,1)S(1)}, u32[]{:S(2)}, u32[]{:S(2)}) collective-permute-start(bf16[4,1,192]{2,1,0:T(2,128)(2,1)S(1)} %get-tuple-element.20), channel_id=1, source_target_pairs={{1,0},{3,2},{5,4},{7,6},{9,8},{11,10},{13,12},{15,14},{17,16},{19,... | collective-permute-start | bytes 4616 | tf_op jit(solution)/shard_map/ppermute | solution.py:15
  37.1 3.8 %collective-permute-start.6 = (bf16[4,1,192]{2,1,0:T(2,128)(2,1)S(1)}, bf16[4,1,192]{2,1,0:T(2,128)(2,1)S(1)}, u32[]{:S(2)}, u32[]{:S(2)}) collective-permute-start(bf16[4,1,192]{2,1,0:T(2,128)(2,1)S(1)} %get-tuple-element.19), channel_id=1, source_target_pairs={{0,1},{2,3},{4,5},{6,7},{8,9},{10,11},{12,13},{14,15},{16,17},{18,... | collective-permute-start | bytes 4616 | tf_op jit(solution)/shard_map/ppermute | solution.py:14
  40.4 7.5 %copy-start.1 = (bf16[768,384]{1,0:T(8,128)(2,1)S(1)}, bf16[768,384]{1,0:T(8,128)(2,1)}, u32[]{:S(2)}) copy-start(bf16[768,384]{1,0:T(8,128)(2,1)} %param.16) | copy-start | bytes 1769476
  41.9 0.7 %copy-start.3 = (f32[192]{0:T(256)S(1)}, f32[192]{0:T(256)}, u32[]{:S(2)}) copy-start(f32[192]{0:T(256)} %param.14) | copy-start | bytes 2308
  42.7 4.5 %collective-permute-start.8 = (bf16[16,192]{1,0:T(8,128)(2,1)S(1)}, bf16[16,192]{1,0:T(8,128)(2,1)S(1)}, u32[]{:S(2)}, u32[]{:S(2)}) collective-permute-start(bf16[16,192]{1,0:T(8,128)(2,1)S(1)} %multiply_convert_fusion.3), channel_id=1, source_target_pairs={{0,2},{2,0},{4,6},{6,4},{8,10},{10,8},{12,14},{14,12},{1,3},{3,1},... | collective-permute-start | bytes 18440 | tf_op jit(solution)/shard_map/ppermute | solution.py:27
  49.1 3.7 %collective-permute-start.9 = (bf16[16,192]{1,0:T(8,128)(2,1)S(1)}, bf16[16,192]{1,0:T(8,128)(2,1)S(1)}, u32[]{:S(2)}, u32[]{:S(2)}) collective-permute-start(bf16[16,192]{1,0:T(8,128)(2,1)S(1)} %multiply_convert_fusion.2), channel_id=1, source_target_pairs={{0,4},{4,0},{2,6},{6,2},{8,12},{12,8},{10,14},{14,10},{1,5},{5,1},... | collective-permute-start | bytes 18440 | tf_op jit(solution)/shard_map/ppermute | solution.py:27
  54.6 4.6 %collective-permute-start.10 = (bf16[16,192]{1,0:T(8,128)(2,1)S(1)}, bf16[16,192]{1,0:T(8,128)(2,1)S(1)}, u32[]{:S(2)}, u32[]{:S(2)}) collective-permute-start(bf16[16,192]{1,0:T(8,128)(2,1)S(1)} %multiply_convert_fusion.1), channel_id=1, source_target_pairs={{0,8},{8,0},{2,10},{10,2},{4,12},{12,4},{6,14},{14,6},{1,9},{9,1},... | collective-permute-start | bytes 18440 | tf_op jit(solution)/shard_map/ppermute | solution.py:27
  61.1 1.2 %collective-permute-start.11 = (bf16[16,192]{1,0:T(8,128)(2,1)S(1)}, bf16[16,192]{1,0:T(8,128)(2,1)S(1)}, u32[]{:S(2)}, u32[]{:S(2)}) collective-permute-start(bf16[16,192]{1,0:T(8,128)(2,1)S(1)} %multiply_convert_fusion), channel_id=1, source_target_pairs={{0,1},{1,0},{2,3},{3,2},{4,5},{5,4},{6,7},{7,6},{8,9},{9,8},{10,11... | collective-permute-start | bytes 18440 | tf_op jit(solution)/shard_map/ppermute | solution.py:27
where the time goes:
time: 65.1 us; the launch traced here: 64.5 us
  starting transfers between devices  27.7 us (43%)
  matrix products  13.3 us (20%)
  waiting for transfers between devices  11.8 us (18%)
  local copies, waits for them, and re-layouts  8.77 us (13%)
  other arithmetic  2.53 us (4%)
    ppermute x4, starting transfers between devices, with_halo(): before = lax.ppermute(last, axis, up)  15.4 us
    dot_general x18, matrix products, convolve(): jnp.dot(window, kernel[row_shift, col_shift], preferred_element_type=jnp....  10.7 us
    ppermute x4, starting transfers between devices, swapped(): return lax.ppermute(block, axis, route)  7.11 us
    ppermute x4, waiting for transfers between devices, swapped(): return lax.ppermute(block, axis, route)  6.79 us
    ppermute x4, starting transfers between devices, with_halo(): after = lax.ppermute(first, axis, down)  5.17 us
    ppermute x4, waiting for transfers between devices, with_halo(): after = lax.ppermute(first, axis, down)  4.5 us
    scatter x4, local copies, waits for them, and re-layouts, switch_level(): jnp.zeros_like(order).at[order].set(jnp.arange(cell_count, dtype=jnp.int32))  2.49 us
    gather x4, local copies, waits for them, and re-layouts, switch_level(): pair_units = jnp.concatenate([lower_part, upper_part[order]], axis=1)  2.35 us
  transfers between devices with their start and end apart: 12, of which 6 were waited for; matrix products, arithmetic and copies ran while one was open for 14% of the time, Pallas kernels for 0%

commit v1 on v0

--- a/solution.py
+++ b/solution.py
@@ -1,7 +1,280 @@
+import functools
+
 import jax
 import jax.numpy as jnp
 from jax import lax
+from jax.experimental import pallas as pl
+from jax.experimental.pallas import tpu as pltpu
 from jax.sharding import PartitionSpec as P
+
+MESH = pl.DeviceIdType.MESH
+
+
+def window_kernel(
+    n_row,
+    n_col,
+    tile_rows,
+    tile_cols,
+    feats_hbm,
+    class_hbm,
+    table_hbm,
+    one_hbm,
+    two_hbm,
+    gain_hbm,
+    w_in_hbm,
+    w_out_hbm,
+    perm_hbm,
+    out_ref,
+    feats,
+    classes,
+    table,
+    kernel_one,
+    kernel_two,
+    gain,
+    w_in,
+    w_out,
+    perm,
+    w_out_half,
+    embedded,
+    tiles,
+    window,
+    shifted,
+    local_sem,
+    send_sem,
+    recv_sem,
+):
+    f32, bf16, i32 = jnp.float32, jnp.bfloat16, jnp.int32
+    count = n_row * n_col
+    cells = tile_rows * tile_cols
+    channels = feats.shape[2]
+    width = n_col * tile_cols
+    total = count * cells
+    row_bits = n_row.bit_length() - 1
+    col_bits = n_col.bit_length() - 1
+    levels = row_bits + col_bits
+    row = lax.axis_index("row")
+    col = lax.axis_index("col")
+    me = row * n_col + col
+
+    moves = [
+        pltpu.make_async_copy(src, dst, local_sem.at[i])
+        for i, (src, dst) in enumerate(
+            (
+                (class_hbm, classes),
+                (feats_hbm, feats),
+                (table_hbm, table),
+                (perm_hbm, perm),
+                (w_out_hbm, w_out),
+                (one_hbm, kernel_one),
+                (two_hbm, kernel_two),
+                (gain_hbm, gain),
+                (w_in_hbm, w_in),
+            )
+        )
+    ]
+    for move in moves[:3]:
+        move.start()
+
+    def peer(apart):
+        other = lax.rem(me + apart, count)
+        return {"row": other // n_col, "col": lax.rem(other, n_col)}
+
+    barrier = pltpu.get_barrier_semaphore()
+    for apart in range(1, count):
+        pl.semaphore_signal(barrier, inc=1, device_id=peer(apart), device_id_type=MESH)
+    for move in moves[3:]:
+        move.start()
+    for move in moves[:3]:
+        move.wait()
+
+    for r in range(tile_rows):
+        for c in range(tile_cols):
+            embedded[pl.ds(r * tile_cols + c, 1), :] = table[pl.ds(classes[r, c], 1), :]
+    initial = feats[...].reshape(cells, channels) + embedded[...]
+    rounded = initial.astype(bf16)
+    tiles[me] = rounded
+    own_rest = initial - rounded.astype(f32)
+
+    pl.semaphore_wait(barrier, count - 1)
+    sends = []
+    for apart in range(1, count):
+        copy = pltpu.make_async_remote_copy(
+            src_ref=tiles.at[me],
+            dst_ref=tiles.at[me],
+            send_sem=send_sem.at[apart - 1],
+            recv_sem=recv_sem.at[apart - 1],
+            device_id=peer(apart),
+            device_id_type=MESH,
+        )
+        copy.start()
+        sends.append(copy)
+
+    moves[3].wait()
+    ups = [(row // (1 << bit)) % 2 for bit in range(row_bits)]
+    ups += [(col // (1 << bit)) % 2 for bit in range(col_bits)]
+    down_iota = lax.broadcasted_iota(i32, (cells, cells), 0)
+    across_iota = lax.broadcasted_iota(i32, (cells, cells), 1)
+    picks = []
+    for level in range(levels):
+        upper = jnp.broadcast_to(ups[level], (cells, cells)) == 1
+        place = jnp.where(upper, across_iota, down_iota)
+        target = jnp.where(upper, down_iota, across_iota)
+        value = jnp.zeros((cells, cells), i32)
+        for k in range(cells):
+            value = jnp.where(place == k, perm[level, k], value)
+        picks.append(jnp.where(value == target, 1.0, 0.0).astype(bf16))
+    orders = jnp.where(down_iota == across_iota, 1.0, 0.0).astype(bf16)
+    for level in reversed(range(levels)):
+        turned = jnp.dot(orders, picks[level], preferred_element_type=f32).astype(bf16)
+        orders = jnp.concatenate([orders, turned], axis=0)
+    cell_iota = lax.broadcasted_iota(i32, (cells, total), 0)
+    spot = lax.broadcasted_iota(i32, (cells, total), 1)
+    spot_cell = ((spot // width) % tile_rows) * tile_cols + spot % tile_cols
+    spread = jnp.where(cell_iota == spot_cell, 1.0, 0.0).astype(bf16)
+    order_rows = jnp.dot(orders, spread, preferred_element_type=f32)
+    place = lax.broadcasted_iota(i32, (total, 1), 0) // cells
+    row_mask = jnp.zeros((total, 1), i32)
+    col_mask = jnp.zeros((total, 1), i32)
+    for level in range(levels):
+        bit = (place >> (levels - 1 - level)) & 1
+        if level < row_bits:
+            row_mask = row_mask | (bit << level)
+        else:
+            col_mask = col_mask | (bit << (level - row_bits))
+    tile_at = (row ^ row_mask) * n_col + (col ^ col_mask)
+    spot_line = lax.broadcasted_iota(i32, (1, total), 1)
+    spot_tile = (spot_line // (width * tile_rows)) * n_col + (spot_line % width) // tile_cols
+    gather = jnp.where(tile_at == spot_tile, order_rows, 0.0).astype(bf16)
+
+    moves[4].wait()
+    w_out_half[0] = w_out[:, :channels]
+    w_out_half[1] = w_out[:, channels:]
+    edge = jnp.zeros((width, channels), bf16)
+    for b in range(3):
+        shifted[b, pl.ds(0, width), :] = edge
+        shifted[b, pl.ds(width + total, width), :] = edge
+    for move in moves[5:]:
+        move.wait()
+
+    for copy in sends:
+        copy.wait_recv()
+
+    for tile in range(count):
+        t, s = divmod(tile, n_col)
+        values = tiles[tile].astype(f32)
+        for r in range(tile_rows):
+            at = (t * tile_rows + r) * width + s * tile_cols
+            window[pl.ds(at, tile_cols), :] = values[r * tile_cols : (r + 1) * tile_cols]
+
+    column = lax.broadcasted_iota(i32, (total, 1), 0) % width
+
+    def convolve(values, kernel):
+        before = jnp.where(column == 0, 0.0, pltpu.roll(values, 1, 0))
+        after = jnp.where(column == width - 1, 0.0, pltpu.roll(values, total - 1, 0))
+        for b, part in enumerate((before, values, after)):
+            shifted[b, pl.ds(width, total), :] = part.astype(bf16)
+        summed = None
+        for a in range(3):
+            for b in range(3):
+                term = jnp.dot(
+                    shifted[b, pl.ds(a * width, total), :],
+                    kernel[3 * a + b],
+                    preferred_element_type=f32,
+                )
+                summed = term if summed is None else summed + term
+        return jnp.maximum(summed, 0.0)
+
+    rounded_window = window[...]
+    conv_one = convolve(rounded_window, kernel_one).astype(bf16).astype(f32)
+    stream = rounded_window + convolve(conv_one, kernel_two)
+    high = stream.astype(bf16)
+    low = (stream - high.astype(f32)).astype(bf16)
+    stream = jnp.dot(gather, high, preferred_element_type=f32) + jnp.dot(
+        gather, low, preferred_element_type=f32
+    )
+    own_part = stream[:cells] + own_rest
+    stream = jnp.concatenate([own_part, stream[cells:]], axis=0)
+
+    size = total
+    for level in range(levels):
+        normed = (
+            stream
+            * lax.rsqrt(jnp.mean(stream * stream, axis=-1, keepdims=True) + 1e-05)
+            * gain[...]
+        ).astype(bf16)
+        size = size // 2
+        up = ups[level]
+        hidden = jnp.dot(normed[:size], w_in[up], preferred_element_type=f32) + jnp.dot(
+            normed[size:], w_in[1 - up], preferred_element_type=f32
+        )
+        hidden = jnp.maximum(hidden, 0.0).astype(bf16)
+        stream = stream[:size] + jnp.dot(
+            hidden, w_out_half[up], preferred_element_type=f32
+        )
+    out_ref[...] = stream.reshape(tile_rows, tile_cols, channels)
+    for copy in sends:
+        copy.wait_send()
+
+
+def whole_window(
+    n_row,
+    n_col,
+    pair_feats,
+    pair_class,
+    class_table,
+    kernel_one,
+    kernel_two,
+    norm_gain,
+    w_in,
+    w_out,
+    partner_perm,
+):
+    tile_rows, tile_cols, channels = pair_feats.shape
+    hidden = w_in.shape[1]
+    count = n_row * n_col
+    cells = tile_rows * tile_cols
+    total = count * cells
+    width = n_col * tile_cols
+    f32, bf16 = jnp.float32, jnp.bfloat16
+    anywhere = pl.BlockSpec(memory_space=pltpu.HBM)
+    return pl.pallas_call(
+        functools.partial(window_kernel, n_row, n_col, tile_rows, tile_cols),
+        out_shape=jax.ShapeDtypeStruct(pair_feats.shape, f32),
+        in_specs=[anywhere] * 9,
+        out_specs=pl.BlockSpec(memory_space=pltpu.VMEM),
+        scratch_shapes=[
+            pltpu.VMEM(pair_feats.shape, f32),
+            pltpu.SMEM(pair_class.shape, jnp.int32),
+            pltpu.VMEM(class_table.shape, f32),
+            pltpu.VMEM((9, channels, channels), bf16),
+            pltpu.VMEM((9, channels, channels), bf16),
+            pltpu.VMEM((1, channels), f32),
+            pltpu.VMEM((2, channels, hidden), bf16),
+            pltpu.VMEM(w_out.shape, bf16),
+            pltpu.SMEM(partner_perm.shape, jnp.int32),
+            pltpu.VMEM((2, hidden, channels), bf16),
+            pltpu.VMEM((cells, channels), f32),
+            pltpu.VMEM((count, cells, channels), bf16),
+            pltpu.VMEM((total, channels), f32),
+            pltpu.VMEM((3, total + 2 * width, channels), bf16),
+            pltpu.SemaphoreType.DMA((9,)),
+            pltpu.SemaphoreType.DMA((count - 1,)),
+            pltpu.SemaphoreType.DMA((count - 1,)),
+        ],
+        compiler_params=pltpu.CompilerParams(
+            collective_id=0, has_side_effects=True, vmem_limit_bytes=48 << 20
+        ),
+    )(
+        pair_feats,
+        pair_class,
+        class_table,
+        kernel_one.reshape(9, channels, channels),
+        kernel_two.reshape(9, channels, channels),
+        norm_gain.reshape(1, channels),
+        w_in.reshape(2, channels, hidden),
+        w_out,
+        partner_perm,
+    )
 
 
 def with_halo(x, sides, width):
@@ -76,7 +349,7 @@
     return stream + update
 
 
-def per_device(
+def tile_by_tile(
     pair_feats,
     pair_class,
     class_table,
@@ -114,9 +387,18 @@
     return stream.reshape(tile_rows, tile_cols, channels)
 
 
+def per_device(n_row, n_col, *operands):
+    tile_rows, tile_cols, channels = operands[0].shape
+    cells = tile_rows * tile_cols
+    window_cells = n_row * n_col * cells
+    if window_cells <= 512 and tile_cols % 8 == 0 and cells % 16 == 0:
+        return whole_window(n_row, n_col, *operands)
+    return tile_by_tile(*operands)
+
+
 def solution(mesh):
     return jax.shard_map(
-        per_device,
+        functools.partial(per_device, mesh.shape["row"], mesh.shape["col"]),
         mesh=mesh,
         in_specs=(
             P(("grp", "row"), "col", None),

time: 65.1 us -> 21 us (0.32)
  starting transfers between devices: 27.7 us -> 0 us
  matrix products: 13.3 us -> 0 us
  Pallas kernels: 0 us -> 13.3 us
  waiting for transfers between devices: 11.8 us -> 0 us
  other arithmetic: 2.53 us -> 0 us
  local copies, waits for them, and re-layouts: 8.77 us -> 7.33 us
    ppermute x12 -> x0, starting transfers between devices: 27.7 us -> none  [the longest x4 15.4 us: with_halo(): before = lax.ppermute(last, axis, up)]
    dot_general x23 -> x0, matrix products: 13.3 us -> none  [the longest x18 10.7 us: convolve(): jnp.dot(window, kernel[row_shift, col_shift], preferred_element_type=jnp....]
    pallas_call x0 -> x1, Pallas kernels: none -> 13.3 us  [whole_window(): pl.pallas_call(functools.partial(window_kernel, n_row, n_col, tile_rows,...]
    ppermute x12 -> x0, waiting for transfers between devices: 11.8 us -> none  [the longest x4 6.79 us: swapped(): return lax.ppermute(block, axis, route)]
    unnamed x8 -> x19, local copies, waits for them, and re-layouts: 0.69 us -> 7.33 us
    gather x8 -> x0, local copies, waits for them, and re-layouts: 4.7 us -> none  [the longest x4 2.35 us: switch_level(): pair_units = jnp.concatenate([lower_part, upper_part[order]], axis=1)]
    scatter x4 -> x0, local copies, waits for them, and re-layouts: 2.49 us -> none  [switch_level(): jnp.zeros_like(order).at[order].set(jnp.arange(cell_count, dtype=jnp.int32))]
    select_n x9 -> x0, other arithmetic: 1.16 us -> none  [the longest x1 0.84 us: switch_level(): pair_units = jnp.concatenate([lower_part, upper_part[order]], axis=1)]
  transfers between devices with their start and end apart: 12 -> 0, of which waited for: 6 -> 0; matrix products, arithmetic and copies ran while one was open for 14% -> 0% of each run, Pallas kernels for 0% -> 0%
where the time goes in v1:
time: 21 us; the launch traced here: 20.6 us
  Pallas kernels  13.3 us (63%)
  local copies, waits for them, and re-layouts  7.33 us (35%)
    pallas_call x1, Pallas kernels, whole_window(): pl.pallas_call(functools.partial(window_kernel, n_row, n_col, tile_rows,...  13.3 us
    unnamed x19, local copies, waits for them, and re-layouts  7.33 us

profile of v1, /device:TPU:0, one launch (start us, length us, event | category | flops | bytes accessed | tf_op | source)
XLA Modules:
  0.0 20.6 jit_solution(8571962554860319120)
XLA Ops:
  0.0 0.0 copy-start.8
  0.0 0.0 copy-start.6
  0.0 0.0 copy-start.7
  0.0 0.7 %copy-done.8 = f32[192]{0:T(256)S(1)} copy-done((f32[192]{0:T(256)S(1)}, f32[192]{0:T(256)}, u32[]{:S(2)}) %copy-start.8) | copy-done | bytes 792
  0.7 0.0 copy-done.6
  0.7 0.0 copy-done.7
  0.7 0.0 copy-start
  0.7 1.2 %copy-done = bf16[3,3,192,192]{3,2,1,0:T(8,128)(2,1)S(1)} copy-done((bf16[3,3,192,192]{3,2,1,0:T(8,128)(2,1)S(1)}, bf16[3,3,192,192]{3,2,1,0:T(8,128)(2,1)}, u32[]{:S(2)}) %copy-start) | copy-done | bytes 663576
  1.9 0.0 copy-start.1
  1.9 1.2 %copy-done.1 = bf16[3,3,192,192]{3,2,1,0:T(8,128)(2,1)S(1)} copy-done((bf16[3,3,192,192]{3,2,1,0:T(8,128)(2,1)S(1)}, bf16[3,3,192,192]{3,2,1,0:T(8,128)(2,1)}, u32[]{:S(2)}) %copy-start.1) | copy-done | bytes 663576
  3.0 0.0 copy-start.2
  3.0 1.1 %copy-done.2 = bf16[384,768]{1,0:T(8,128)(2,1)S(1)} copy-done((bf16[384,768]{1,0:T(8,128)(2,1)S(1)}, bf16[384,768]{1,0:T(8,128)(2,1)}, u32[]{:S(2)}) %copy-start.2) | copy-done | bytes 589848
  4.1 0.0 copy-start.3
  4.1 1.1 %copy-done.3 = bf16[768,384]{1,0:T(8,128)(2,1)S(1)} copy-done((bf16[768,384]{1,0:T(8,128)(2,1)S(1)}, bf16[768,384]{1,0:T(8,128)(2,1)}, u32[]{:S(2)}) %copy-start.3) | copy-done | bytes 589848
  5.2 0.0 copy-start.4
  5.2 0.8 %copy-done.4 = f32[64,192]{1,0:T(8,128)S(1)} copy-done((f32[64,192]{1,0:T(8,128)S(1)}, f32[64,192]{1,0:T(8,128)}, u32[]{:S(2)}) %copy-start.4) | copy-done | bytes 49176
  6.0 0.0 copy-start.5
  6.0 0.7 %copy-done.5 = f32[2,8,192]{2,1,0:T(8,128)S(1)} copy-done((f32[2,8,192]{2,1,0:T(8,128)S(1)}, f32[2,8,192]{2,1,0:T(8,128)}, u32[]{:S(2)}) %copy-start.5) | copy-done | bytes 12312
  6.7 13.3 %shard_map.91 = f32[2,8,192]{2,1,0:T(8,128)S(1)} custom-call(f32[2,8,192]{2,1,0:T(8,128)S(1)} %copy-done.5, s32[2,8]{1,0:T(2,128)S(1)} %copy-done.7, f32[64,192]{1,0:T(8,128)S(1)} %copy-done.4, bf16[9,192,192]{2,1,0:T(8,128)(2,1)S(1)} %bitcast.4, bf16[9,192,192]{2,1,0:T(8,128)(2,1)S(1)} %bitcast.5, f32[1,192]{1,0:T(1,128)S(1)} %bitcast.7, ...), custom_call_target="tpu_custom_call" | custom-call | tf_op jit(solution)/shard_map/pallas_call | solution.py:240
  20.0 0.6 %copy.11 = f32[2,8,192]{2,1,0:T(8,128)} copy(f32[2,8,192]{2,1,0:T(8,128)S(1)} %shard_map.91) | data formatting | bytes 24576
Async XLA Ops:
  0.0 0.7 %copy-start.8 = (f32[192]{0:T(256)S(1)}, f32[192]{0:T(256)}, u32[]{:S(2)}) copy-start(f32[192]{0:T(256)} %param.14) | copy-start | bytes 2308
  0.0 0.7 %copy-start.6 = (s32[4,16]{1,0:T(4,128)S(1)}, s32[4,16]{1,0:T(4,128)}, u32[]{:S(2)}) copy-start(s32[4,16]{1,0:T(4,128)} %perm_hbm.1) | copy-start | bytes 772
  0.0 0.7 %copy-start.7 = (s32[2,8]{1,0:T(2,128)S(1)}, s32[2,8]{1,0:T(2,128)}, u32[]{:S(2)}) copy-start(s32[2,8]{1,0:T(2,128)} %class_hbm.1) | copy-start | bytes 196
  0.7 1.2 %copy-start = (bf16[3,3,192,192]{3,2,1,0:T(8,128)(2,1)S(1)}, bf16[3,3,192,192]{3,2,1,0:T(8,128)(2,1)}, u32[]{:S(2)}) copy-start(bf16[3,3,192,192]{3,2,1,0:T(8,128)(2,1)} %param.12) | copy-start | bytes 1990660
  1.9 1.2 %copy-start.1 = (bf16[3,3,192,192]{3,2,1,0:T(8,128)(2,1)S(1)}, bf16[3,3,192,192]{3,2,1,0:T(8,128)(2,1)}, u32[]{:S(2)}) copy-start(bf16[3,3,192,192]{3,2,1,0:T(8,128)(2,1)} %param.13) | copy-start | bytes 1990660
  3.0 1.1 %copy-start.2 = (bf16[384,768]{1,0:T(8,128)(2,1)S(1)}, bf16[384,768]{1,0:T(8,128)(2,1)}, u32[]{:S(2)}) copy-start(bf16[384,768]{1,0:T(8,128)(2,1)} %param.15) | copy-start | bytes 1769476
  4.1 1.1 %copy-start.3 = (bf16[768,384]{1,0:T(8,128)(2,1)S(1)}, bf16[768,384]{1,0:T(8,128)(2,1)}, u32[]{:S(2)}) copy-start(bf16[768,384]{1,0:T(8,128)(2,1)} %w_out_hbm.1) | copy-start | bytes 1769476
  5.2 0.8 %copy-start.4 = (f32[64,192]{1,0:T(8,128)S(1)}, f32[64,192]{1,0:T(8,128)}, u32[]{:S(2)}) copy-start(f32[64,192]{1,0:T(8,128)} %table_hbm.1) | copy-start | bytes 147460
  6.0 0.7 %copy-start.5 = (f32[2,8,192]{2,1,0:T(8,128)S(1)}, f32[2,8,192]{2,1,0:T(8,128)}, u32[]{:S(2)}) copy-start(f32[2,8,192]{2,1,0:T(8,128)} %feats_hbm.1) | copy-start | bytes 36868

commit v2 on v1

--- a/solution.py
+++ b/solution.py
@@ -262,7 +262,7 @@
             pltpu.SemaphoreType.DMA((count - 1,)),
         ],
         compiler_params=pltpu.CompilerParams(
-            collective_id=0, has_side_effects=True, vmem_limit_bytes=48 << 20
+            collective_id=0, has_side_effects=True, vmem_limit_bytes=62 << 20
         ),
     )(
         pair_feats,

time: 21 us -> 15.3 us (0.73)
  local copies, waits for them, and re-layouts: 7.33 us -> 1.32 us
  Pallas kernels: 13.3 us -> 13.7 us
    unnamed x19 -> x1, local copies, waits for them, and re-layouts: 7.33 us -> 1.32 us
    pallas_call x1, Pallas kernels: 13.3 us -> 13.7 us  [whole_window(): pl.pallas_call(functools.partial(window_kernel, n_row, n_col, tile_rows,...]
where the time goes in v2:
time: 15.3 us; the launch traced here: 15 us
  Pallas kernels  13.7 us (90%)
  local copies, waits for them, and re-layouts  1.32 us (9%)
    pallas_call x1, Pallas kernels, whole_window(): pl.pallas_call(functools.partial(window_kernel, n_row, n_col, tile_rows,...  13.7 us
    unnamed x1, local copies, waits for them, and re-layouts  1.32 us

profile of v2, /device:TPU:0, one launch (start us, length us, event | category | flops | bytes accessed | tf_op | source)
XLA Modules:
  0.0 15.0 jit_solution(12976451182522545605)
XLA Ops:
  0.0 13.7 %shard_map.91 = f32[2,8,192]{2,1,0:T(8,128)} custom-call(f32[2,8,192]{2,1,0:T(8,128)} %feats_hbm.1, s32[2,8]{1,0:T(2,128)} %class_hbm.1, f32[64,192]{1,0:T(8,128)} %table_hbm.1, bf16[9,192,192]{2,1,0:T(8,128)(2,1)} %bitcast.4, bf16[9,192,192]{2,1,0:T(8,128)(2,1)} %bitcast.5, f32[1,192]{1,0:T(1,128)} %bitcast.7, bf16[2,192,768]{2,1,0:T(8,128)(2,1)} %bitcast.6, ...), custom_call_target="tpu_custom_call" | custom-call | tf_op jit(solution)/shard_map/pallas_call | solution.py:240
  13.7 1.3 %copy.11 = f32[2,8,192]{2,1,0:T(8,128)} copy(f32[2,8,192]{2,1,0:T(8,128)} %shard_map.91) | data formatting | bytes 24576

commit v3 on v2

--- a/solution.py
+++ b/solution.py
@@ -197,16 +197,13 @@
 
     size = total
     for level in range(levels):
-        normed = (
-            stream
-            * lax.rsqrt(jnp.mean(stream * stream, axis=-1, keepdims=True) + 1e-05)
-            * gain[...]
-        ).astype(bf16)
+        scaled = (stream * gain[...]).astype(bf16)
+        rate = lax.rsqrt(jnp.mean(stream * stream, axis=-1, keepdims=True) + 1e-05)
         size = size // 2
         up = ups[level]
-        hidden = jnp.dot(normed[:size], w_in[up], preferred_element_type=f32) + jnp.dot(
-            normed[size:], w_in[1 - up], preferred_element_type=f32
-        )
+        hidden = rate[:size] * jnp.dot(
+            scaled[:size], w_in[up], preferred_element_type=f32
+        ) + rate[size:] * jnp.dot(scaled[size:], w_in[1 - up], preferred_element_type=f32)
         hidden = jnp.maximum(hidden, 0.0).astype(bf16)
         stream = stream[:size] + jnp.dot(
             hidden, w_out_half[up], preferred_element_type=f32
@@ -239,7 +236,7 @@
     anywhere = pl.BlockSpec(memory_space=pltpu.HBM)
     return pl.pallas_call(
         functools.partial(window_kernel, n_row, n_col, tile_rows, tile_cols),
-        out_shape=jax.ShapeDtypeStruct(pair_feats.shape, f32),
+        out_shape=pltpu.VMEM(pair_feats.shape, f32),
         in_specs=[anywhere] * 9,
         out_specs=pl.BlockSpec(memory_space=pltpu.VMEM),
         scratch_shapes=[

time: 15.3 us -> 13.5 us (0.88)
  Pallas kernels: 13.7 us -> 12.7 us
  local copies, waits for them, and re-layouts: 1.32 us -> 0.61 us
    pallas_call x1, Pallas kernels: 13.7 us -> 12.7 us  [whole_window(): pl.pallas_call(functools.partial(window_kernel, n_row, n_col, tile_rows,...]
    unnamed x1, local copies, waits for them, and re-layouts: 1.32 us -> 0.61 us
where the time goes in v3:
time: 13.5 us; the launch traced here: 13.3 us
  Pallas kernels  12.7 us (94%)
  local copies, waits for them, and re-layouts  0.61 us (5%)
    pallas_call x1, Pallas kernels, whole_window(): pl.pallas_call(functools.partial(window_kernel, n_row, n_col, tile_rows,...  12.7 us
    unnamed x1, local copies, waits for them, and re-layouts  0.61 us

profile of v3, /device:TPU:0, one launch (start us, length us, event | category | flops | bytes accessed | tf_op | source)
XLA Modules:
  0.0 13.3 jit_solution(7060268552152171499)
XLA Ops:
  0.0 12.7 %shard_map.91 = f32[2,8,192]{2,1,0:T(8,128)S(1)} custom-call(f32[2,8,192]{2,1,0:T(8,128)} %feats_hbm.1, s32[2,8]{1,0:T(2,128)} %class_hbm.1, f32[64,192]{1,0:T(8,128)} %table_hbm.1, bf16[9,192,192]{2,1,0:T(8,128)(2,1)} %bitcast.4, bf16[9,192,192]{2,1,0:T(8,128)(2,1)} %bitcast.5, f32[1,192]{1,0:T(1,128)} %bitcast.7, bf16[2,192,768]{2,1,0:T(8,128)(2,1)} %bitcast.6, ...), custom_call_target="tpu_custom_call" | custom-call | tf_op jit(solution)/shard_map/pallas_call | solution.py:237
  12.7 0.6 %copy.11 = f32[2,8,192]{2,1,0:T(8,128)} copy(f32[2,8,192]{2,1,0:T(8,128)S(1)} %shard_map.91) | data formatting | bytes 24576

commit v4 on v3

--- a/solution.py
+++ b/solution.py
@@ -38,6 +38,7 @@
     embedded,
     tiles,
     window,
+    columns,
     shifted,
     local_sem,
     send_sem,
@@ -96,18 +97,29 @@
     own_rest = initial - rounded.astype(f32)
 
     pl.semaphore_wait(barrier, count - 1)
+    others = [i + (i - me + count) // count for i in range(count - 1)]
     sends = []
-    for apart in range(1, count):
+    for i, other in enumerate(others):
         copy = pltpu.make_async_remote_copy(
             src_ref=tiles.at[me],
             dst_ref=tiles.at[me],
-            send_sem=send_sem.at[apart - 1],
-            recv_sem=recv_sem.at[apart - 1],
-            device_id=peer(apart),
+            send_sem=send_sem.at[i],
+            recv_sem=recv_sem.at[me],
+            device_id={"row": other // n_col, "col": lax.rem(other, n_col)},
             device_id_type=MESH,
         )
         copy.start()
         sends.append(copy)
+
+    def arrived(tile):
+        pltpu.make_async_remote_copy(
+            src_ref=tiles.at[tile],
+            dst_ref=tiles.at[tile],
+            send_sem=send_sem.at[0],
+            recv_sem=recv_sem.at[tile],
+            device_id={"row": tile // n_col, "col": lax.rem(tile, n_col)},
+            device_id_type=MESH,
+        ).wait_recv()
 
     moves[3].wait()
     ups = [(row // (1 << bit)) % 2 for bit in range(row_bits)]
@@ -156,8 +168,8 @@
     for move in moves[5:]:
         move.wait()
 
-    for copy in sends:
-        copy.wait_recv()
+    for other in others:
+        arrived(other)
 
     for tile in range(count):
         t, s = divmod(tile, n_col)
@@ -173,15 +185,12 @@
         after = jnp.where(column == width - 1, 0.0, pltpu.roll(values, total - 1, 0))
         for b, part in enumerate((before, values, after)):
             shifted[b, pl.ds(width, total), :] = part.astype(bf16)
-        summed = None
         for a in range(3):
             for b in range(3):
-                term = jnp.dot(
-                    shifted[b, pl.ds(a * width, total), :],
-                    kernel[3 * a + b],
-                    preferred_element_type=f32,
-                )
-                summed = term if summed is None else summed + term
+                columns[:, pl.ds((3 * a + b) * channels, channels)] = shifted[
+                    b, pl.ds(a * width, total), :
+                ]
+        summed = jnp.dot(columns[...], kernel[...], preferred_element_type=f32)
         return jnp.maximum(summed, 0.0)
 
     rounded_window = window[...]
@@ -189,10 +198,10 @@
     stream = rounded_window + convolve(conv_one, kernel_two)
     high = stream.astype(bf16)
     low = (stream - high.astype(f32)).astype(bf16)
-    stream = jnp.dot(gather, high, preferred_element_type=f32) + jnp.dot(
-        gather, low, preferred_element_type=f32
-    )
-    own_part = stream[:cells] + own_rest
+    stream = jnp.dot(gather, high, preferred_element_type=f32)
+    own_part = stream[:cells] + (
+        jnp.dot(gather[:cells], low, preferred_element_type=f32) + own_rest
+    )
     stream = jnp.concatenate([own_part, stream[cells:]], axis=0)
 
     size = total
@@ -243,8 +252,8 @@
             pltpu.VMEM(pair_feats.shape, f32),
             pltpu.SMEM(pair_class.shape, jnp.int32),
             pltpu.VMEM(class_table.shape, f32),
-            pltpu.VMEM((9, channels, channels), bf16),
-            pltpu.VMEM((9, channels, channels), bf16),
+            pltpu.VMEM((9 * channels, channels), bf16),
+            pltpu.VMEM((9 * channels, channels), bf16),
             pltpu.VMEM((1, channels), f32),
             pltpu.VMEM((2, channels, hidden), bf16),
             pltpu.VMEM(w_out.shape, bf16),
@@ -253,10 +262,11 @@
             pltpu.VMEM((cells, channels), f32),
             pltpu.VMEM((count, cells, channels), bf16),
             pltpu.VMEM((total, channels), f32),
+            pltpu.VMEM((total, 9 * channels), bf16),
             pltpu.VMEM((3, total + 2 * width, channels), bf16),
             pltpu.SemaphoreType.DMA((9,)),
             pltpu.SemaphoreType.DMA((count - 1,)),
-            pltpu.SemaphoreType.DMA((count - 1,)),
+            pltpu.SemaphoreType.DMA((count,)),
         ],
         compiler_params=pltpu.CompilerParams(
             collective_id=0, has_side_effects=True, vmem_limit_bytes=62 << 20
@@ -265,8 +275,8 @@
         pair_feats,
         pair_class,
         class_table,
-        kernel_one.reshape(9, channels, channels),
-        kernel_two.reshape(9, channels, channels),
+        kernel_one.reshape(9 * channels, channels),
+        kernel_two.reshape(9 * channels, channels),
         norm_gain.reshape(1, channels),
         w_in.reshape(2, channels, hidden),
         w_out,

time: 13.5 us -> 13.4 us (level)
  no operation moved by 1% of the time
where the time goes in v4:
time: 13.4 us; the launch traced here: 13.3 us
  Pallas kernels  12.6 us (94%)
  local copies, waits for them, and re-layouts  0.61 us (5%)
    pallas_call x1, Pallas kernels, whole_window(): pl.pallas_call(functools.partial(window_kernel, n_row, n_col, tile_rows,...  12.6 us
    unnamed x1, local copies, waits for them, and re-layouts  0.61 us

profile of v4, /device:TPU:0, one launch (start us, length us, event | category | flops | bytes accessed | tf_op | source)
XLA Modules:
  0.0 13.3 jit_solution(13492471414142210910)
XLA Ops:
  0.0 12.6 %shard_map.91 = f32[2,8,192]{2,1,0:T(8,128)S(1)} custom-call(f32[2,8,192]{2,1,0:T(8,128)} %feats_hbm.1, s32[2,8]{1,0:T(2,128)} %class_hbm.1, f32[64,192]{1,0:T(8,128)} %table_hbm.1, bf16[1728,192]{1,0:T(8,128)(2,1)} %bitcast.4, bf16[1728,192]{1,0:T(8,128)(2,1)} %bitcast.5, f32[1,192]{1,0:T(1,128)} %bitcast.7, bf16[2,192,768]{2,1,0:T(8,128)(2,1)} %bitcast.6, ...), custom_call_target="tpu_custom_call" | custom-call | tf_op jit(solution)/shard_map/pallas_call | solution.py:246
  12.6 0.6 %copy.11 = f32[2,8,192]{2,1,0:T(8,128)} copy(f32[2,8,192]{2,1,0:T(8,128)S(1)} %shard_map.91) | data formatting | bytes 24576

commit v5 on v4

--- a/solution.py
+++ b/solution.py
@@ -76,13 +76,14 @@
     for move in moves[:3]:
         move.start()
 
-    def peer(apart):
-        other = lax.rem(me + apart, count)
-        return {"row": other // n_col, "col": lax.rem(other, n_col)}
+    others = [i + (i - me + count) // count for i in range(count - 1)]
+
+    def place_of(tile):
+        return {"row": tile // n_col, "col": lax.rem(tile, n_col)}
 
     barrier = pltpu.get_barrier_semaphore()
-    for apart in range(1, count):
-        pl.semaphore_signal(barrier, inc=1, device_id=peer(apart), device_id_type=MESH)
+    for other in others:
+        pl.semaphore_signal(barrier, inc=1, device_id=place_of(other), device_id_type=MESH)
     for move in moves[3:]:
         move.start()
     for move in moves[:3]:
@@ -97,7 +98,6 @@
     own_rest = initial - rounded.astype(f32)
 
     pl.semaphore_wait(barrier, count - 1)
-    others = [i + (i - me + count) // count for i in range(count - 1)]
     sends = []
     for i, other in enumerate(others):
         copy = pltpu.make_async_remote_copy(

time: 13.4 us -> 13.4 us (level)
  no operation moved by 1% of the time
where the time goes in v5:
time: 13.4 us; the launch traced here: 13.2 us
  Pallas kernels  12.6 us (94%)
  local copies, waits for them, and re-layouts  0.61 us (5%)
    pallas_call x1, Pallas kernels, whole_window(): pl.pallas_call(functools.partial(window_kernel, n_row, n_col, tile_rows,...  12.6 us
    unnamed x1, local copies, waits for them, and re-layouts  0.61 us

profile of v5, /device:TPU:0, one launch (start us, length us, event | category | flops | bytes accessed | tf_op | source)
XLA Modules:
  0.0 13.2 jit_solution(4551144545917245596)
XLA Ops:
  0.0 12.6 %shard_map.91 = f32[2,8,192]{2,1,0:T(8,128)S(1)} custom-call(f32[2,8,192]{2,1,0:T(8,128)} %feats_hbm.1, s32[2,8]{1,0:T(2,128)} %class_hbm.1, f32[64,192]{1,0:T(8,128)} %table_hbm.1, bf16[1728,192]{1,0:T(8,128)(2,1)} %bitcast.4, bf16[1728,192]{1,0:T(8,128)(2,1)} %bitcast.5, f32[1,192]{1,0:T(1,128)} %bitcast.7, bf16[2,192,768]{2,1,0:T(8,128)(2,1)} %bitcast.6, ...), custom_call_target="tpu_custom_call" | custom-call | tf_op jit(solution)/shard_map/pallas_call | solution.py:246
  12.6 0.6 %copy.11 = f32[2,8,192]{2,1,0:T(8,128)} copy(f32[2,8,192]{2,1,0:T(8,128)S(1)} %shard_map.91) | data formatting | bytes 24576
